TPU v7x, 32 devices: a whole 2x2x4 slice. The times are simulated.
32 devices in a mesh: dp: 8 (over y, x, core), tensor: 4 (over z).
Axes of the slice: x: 2, y: 2, z: 4, core: 2. Of those that a mesh axis runs over, the one named last changes fastest.
Arguments:
- inputs: float32 [8192, 1536], P(('dp', 'tensor')), may hold values from -80 to 80
- norm_gains: float32 [1, 2, 1536], replicated, may hold values from 0.5 to 1.5
- w_qkv: bfloat16 [1, 1536, 3072], P(None, 'dp', 'tensor'), may hold values from -0.15625 to 0.15625
- w_gate_up: bfloat16 [1, 1536, 2, 4096], P(None, 'dp', None, 'tensor'), may hold values from -0.15625 to 0.15625
- w_out: bfloat16 [1, 1536, 1536], P(None, 'dp', 'tensor'), may hold values from -2.5 to 2.5
- w_down: bfloat16 [1, 1536, 4096], P(None, 'dp', 'tensor'), may hold values from -0.09375 to 0.09375
- segments: int32 [8192], P('dp'), may hold values from 0 to 8, as said below
- positions: int32 [8192], P('dp'), may hold values from 0 to 799, as said below
- cotangent: bfloat16 [8192, 1536], P(('dp', 'tensor')), may hold values from -6 to 6
Outputs:
- output: float32 [8192, 1536], P(('dp', 'tensor'))
- input_grad: float32 [8192, 1536], P(('dp', 'tensor'))
- grad_qkv: float32 [1, 1536, 3072], P(None, 'dp', 'tensor')
- grad_gate_up: float32 [1, 1536, 2, 4096], P(None, 'dp', None, 'tensor')
- grad_out: float32 [1, 1536, 1536], P(None, 'dp', 'tensor')
- grad_down: float32 [1, 1536, 4096], P(None, 'dp', 'tensor')
- grad_gains: float32 [1, 2, 1536], replicated
- rms_stats: float32 [1, 4], replicated
Inputs may be any that keep to these rules, and one draw needn't show every extreme that they name: `segments`: within each group of 1024 consecutive tokens (one index of dp), the tokens form blocks of 32: 24 prompt blocks with segment 0 and one block for each continuation 1 to 8, in a drawn order of blocks. Within a group the prompt's tokens have positions 0 to 767, rising along the group; each continuation's tokens have positions 768 to 799 in order.
All inputs are finite; a program needn't handle non-finite values.
Results may differ from a plain program's by a relative error of at most 0.012.
The roundings to bfloat16 on the way count: a program that leaves them out, or rounds other values in their place, can miss the bound.
Values may be sent and summed in bfloat16 or wider, within the bound.
A program may use at most 192 MiB of HBM per device.

v0:
```python
import jax
import jax.numpy as jnp
from jax import lax
from jax.sharding import PartitionSpec as P

HEADS = 16
KV_HEADS = 8
HEAD_WIDTH = 96
norm_eps = 1e-05
rope_base = 100000.0


def rope_tables(position, head_dim):
    freq_steps = jnp.arange(head_dim // 2, dtype=jnp.float32) * (2.0 / head_dim)
    inverse = jnp.power(rope_base, -freq_steps)
    angles = position.astype(jnp.float32)[:, None] * inverse[None, :]
    return (jnp.cos(angles), jnp.sin(angles))


def rotate(values, cosine_table, sine_table):
    half_dim = values.shape[-1] // 2
    first_half = values[..., :half_dim]
    second_half = values[..., half_dim:]
    return jnp.concatenate(
        [
            first_half * cosine_table - second_half * sine_table,
            second_half * cosine_table + first_half * sine_table,
        ],
        axis=-1,
    )


def visible(query_segment, query_position, key_segment, key_position):
    same_doc = (key_segment[None, :] == 0) | (key_segment[None, :] == query_segment[:, None])
    return same_doc & (key_position[None, :] <= query_position[:, None])


def normalize(values, gain):
    inverse = lax.rsqrt(jnp.mean(values * values, axis=-1, keepdims=True) + norm_eps)
    return (values * inverse * gain, inverse)


def norm_back(values, inverse, gain, grad_normed):
    scaled = grad_normed * gain
    grad_gain = jnp.sum(grad_normed * values * inverse, axis=0)
    grad_values = inverse * scaled - values * inverse**3 * jnp.mean(
        scaled * values, axis=-1, keepdims=True
    )
    return (grad_values, grad_gain)


def spread_rows(values):
    return lax.all_gather(values, "tensor", axis=0, tiled=True)


def collect_rows(values):
    return lax.psum_scatter(values, "tensor", scatter_dimension=0, tiled=True)


def spread_grads(values):
    return lax.all_gather(values, "tensor", axis=0, tiled=True)


def collect_grads(values):
    return lax.psum_scatter(values, "tensor", scatter_dimension=0, tiled=True)


def refold(normed_local, grad_rows):
    return jnp.einsum(
        "td,tc->dc",
        lax.all_gather(normed_local, "tensor", axis=0, tiled=True),
        grad_rows,
        preferred_element_type=jnp.float32,
    )


def per_device(inputs, norm_gains, w_qkv, w_gate_up, w_out, w_down, segments, positions, cotangent):
    layers = w_qkv.shape[0]
    head_dim = HEAD_WIDTH
    repeat = HEADS // KV_HEADS
    kv_local = w_out.shape[2] // (repeat * head_dim)
    ff_local = w_down.shape[2]
    group_len = segments.shape[0]
    blocks = 2
    block_len = group_len // blocks
    score_scale = head_dim ** (-0.5)
    cosine_table, sine_table = rope_tables(positions, head_dim)
    cosine_wide = cosine_table[:, None, None, :]
    sine_wide = sine_table[:, None, None, :]
    block_segments = segments.reshape(blocks, block_len)
    block_positions = positions.reshape(blocks, block_len)
    layer_index = 0
    gathered = (
        lax.all_gather(w_qkv[layer_index], "dp", axis=0, tiled=True),
        lax.all_gather(w_gate_up[layer_index], "dp", axis=0, tiled=True),
        lax.all_gather(w_out[layer_index], "dp", axis=0, tiled=True),
        lax.all_gather(w_down[layer_index], "dp", axis=0, tiled=True),
    )
    qkv_full, gate_up_full, out_full, down_full = gathered
    normed_one, inverse_one = normalize(inputs, norm_gains[layer_index, 0])
    normed_one = normed_one.astype(jnp.bfloat16)
    normed_rows = spread_rows(normed_one)
    joined_rows = jnp.dot(normed_rows, qkv_full, preferred_element_type=jnp.float32)
    joined_rows = joined_rows.reshape(group_len, kv_local, repeat + 2, head_dim)
    query_matrix = rotate(joined_rows[:, :, :repeat], cosine_wide, sine_wide).astype(jnp.bfloat16)
    key_matrix = rotate(joined_rows[:, :, repeat], cosine_wide[:, :, 0], sine_wide[:, :, 0]).astype(
        jnp.bfloat16
    )
    value_matrix = joined_rows[:, :, repeat + 1].astype(jnp.bfloat16)

    def attend_block(block_item):
        query_block, block_segment, block_position = block_item
        allowed = visible(block_segment, block_position, segments, positions)
        attention_scores = (
            jnp.einsum(
                "mely,cey->elmc", query_block, key_matrix, preferred_element_type=jnp.float32
            )
            * score_scale
        )
        attention_scores = jnp.where(allowed[None, None], attention_scores, -1e30)
        row_top = jnp.max(attention_scores, axis=-1, keepdims=True)
        weights = jnp.exp(attention_scores - row_top)
        row_total = jnp.sum(weights, axis=-1, keepdims=True)
        probability_lowered = (weights / row_total).astype(jnp.bfloat16)
        mixed_rows_block = jnp.einsum(
            "zbvq,qzo->vzbo", probability_lowered, value_matrix, preferred_element_type=jnp.float32
        )
        return (mixed_rows_block.astype(jnp.bfloat16), (row_top + jnp.log(row_total))[..., 0])

    mixed_all, log_sums = lax.map(
        attend_block,
        (
            query_matrix.reshape(blocks, block_len, kv_local, repeat, head_dim),
            block_segments,
            block_positions,
        ),
    )
    attended = mixed_all.reshape(group_len, kv_local * repeat * head_dim)
    branch = collect_rows(
        jnp.einsum("tk,dk->td", attended, out_full, preferred_element_type=jnp.float32)
    )
    middle = inputs + branch
    normed_two, inverse_two = normalize(middle, norm_gains[layer_index, 1])
    normed_two = normed_two.astype(jnp.bfloat16)
    ff_kept = None
    normed_rows_two = spread_rows(normed_two)
    gate_up = jnp.einsum(
        "td,dcf->tcf", normed_rows_two, gate_up_full, preferred_element_type=jnp.float32
    )
    product = (jax.nn.silu(gate_up[:, 0]) * gate_up[:, 1]).astype(jnp.bfloat16)
    branch_two = collect_rows(
        jnp.einsum("tf,df->td", product, down_full, preferred_element_type=jnp.float32)
    )
    output = middle + branch_two
    stat_rows = [
        jnp.stack(
            [
                jnp.sum(middle * middle),
                jnp.sum(output * output),
                jnp.sum(branch * branch),
                jnp.sum(branch_two * branch_two),
            ]
        )
    ]
    kept_items = [
        (
            inputs,
            inverse_one,
            normed_one,
            normed_rows,
            middle,
            inverse_two,
            normed_two,
            normed_rows_two,
            query_matrix,
            key_matrix,
            value_matrix,
            attended,
            log_sums,
            gate_up,
            product,
            gathered,
            ff_kept,
        )
    ]
    grad_hidden = cotangent.astype(jnp.float32)
    grad_qkv_list = [None] * layers
    grad_gu_list = [None] * layers
    grad_out_list = [None] * layers
    grad_down_list = [None] * layers
    gain_list = [None] * layers
    for layer_index in reversed(range(layers)):
        (
            hidden_in,
            inverse_one,
            normed_one,
            normed_rows,
            middle,
            inverse_two,
            normed_two,
            normed_rows_two,
            query_matrix,
            key_matrix,
            value_matrix,
            attended,
            log_sums,
            gate_up,
            product,
            gathered,
            ff_kept,
        ) = kept_items[layer_index]
        qkv_full, gate_up_full, out_full, down_full = (
            lax.all_gather(w_qkv[layer_index], "dp", axis=0, tiled=True),
            lax.all_gather(w_gate_up[layer_index], "dp", axis=0, tiled=True),
            lax.all_gather(w_out[layer_index], "dp", axis=0, tiled=True),
            lax.all_gather(w_down[layer_index], "dp", axis=0, tiled=True),
        )
        gate_rows = gate_up[:, 0]
        up_rows = gate_up[:, 1]
        sigmoid_gate = jax.nn.sigmoid(gate_rows)
        grad_two = spread_grads(grad_hidden.astype(jnp.bfloat16))
        grad_product = jnp.einsum(
            "td,df->tf", grad_two, down_full, preferred_element_type=jnp.float32
        )
        grad_down_w = jnp.einsum("td,tf->df", grad_two, product, preferred_element_type=jnp.float32)
        grad_gate = (
            grad_product * up_rows * (sigmoid_gate * (1.0 + gate_rows * (1.0 - sigmoid_gate)))
        )
        grad_up = grad_product * (gate_rows * sigmoid_gate)
        grad_gate_up = jnp.stack([grad_gate, grad_up], axis=1).astype(jnp.bfloat16)
        grad_gu_w = refold(normed_two, grad_gate_up.reshape(group_len, 2 * ff_local)).reshape(
            -1, 2, ff_local
        )
        grad_normed_two = collect_grads(
            jnp.einsum(
                "tcf,dcf->td", grad_gate_up, gate_up_full, preferred_element_type=jnp.float32
            )
        )
        grad_middle, grad_gain_two = norm_back(
            middle, inverse_two, norm_gains[layer_index, 1], grad_normed_two
        )
        grad_middle = grad_middle + grad_hidden
        grad_one = spread_grads(grad_middle.astype(jnp.bfloat16))
        grad_attended = jnp.einsum(
            "td,dk->tk", grad_one, out_full, preferred_element_type=jnp.float32
        ).astype(jnp.bfloat16)
        grad_out_w = jnp.einsum("td,tk->dk", grad_one, attended, preferred_element_type=jnp.float32)

        def back_block(running_grads, block_item):
            grad_keys, grad_values = running_grads
            query_block, block_gradient, block_sums, block_segment, block_position = block_item
            allowed = visible(block_segment, block_position, segments, positions)
            attention_scores = (
                jnp.einsum(
                    "mely,cey->elmc", query_block, key_matrix, preferred_element_type=jnp.float32
                )
                * score_scale
            )
            attention_scores = jnp.where(allowed[None, None], attention_scores, -1e30)
            probability_full = jnp.exp(attention_scores - block_sums[..., None])
            grad_probs = jnp.einsum(
                "mely,cey->elmc", block_gradient, value_matrix, preferred_element_type=jnp.float32
            )
            row_delta = jnp.sum(probability_full * grad_probs, axis=-1, keepdims=True)
            score_gradient = (probability_full * (grad_probs - row_delta)).astype(jnp.bfloat16)
            grad_query = (
                jnp.einsum(
                    "zbvq,qzo->vzbo", score_gradient, key_matrix, preferred_element_type=jnp.float32
                )
                * score_scale
            )
            grad_keys = (
                grad_keys
                + jnp.einsum(
                    "wqpv,pwqo->vwo",
                    score_gradient,
                    query_block,
                    preferred_element_type=jnp.float32,
                )
                * score_scale
            )
            grad_values = grad_values + jnp.einsum(
                "wqpv,pwqo->vwo",
                probability_full.astype(jnp.bfloat16),
                block_gradient,
                preferred_element_type=jnp.float32,
            )
            return ((grad_keys, grad_values), grad_query)

        zero_rows = jnp.zeros((group_len, kv_local, head_dim), jnp.float32)
        (grad_keys, grad_values), grad_query = lax.scan(
            back_block,
            (zero_rows, zero_rows),
            (
                query_matrix.reshape(blocks, block_len, kv_local, repeat, head_dim),
                grad_attended.reshape(blocks, block_len, kv_local, repeat, head_dim),
                log_sums,
                block_segments,
                block_positions,
            ),
        )
        grad_query = rotate(
            grad_query.reshape(group_len, kv_local, repeat, head_dim), cosine_wide, -sine_wide
        )
        grad_keys = rotate(grad_keys, cosine_wide[:, :, 0], -sine_wide[:, :, 0])
        grad_joined = jnp.concatenate(
            [grad_query, grad_keys[:, :, None], grad_values[:, :, None]], axis=2
        )
        grad_joined = grad_joined.reshape(group_len, kv_local * (repeat + 2) * head_dim).astype(
            jnp.bfloat16
        )
        grad_qkv_w = refold(normed_one, grad_joined)
        grad_normed_one = collect_grads(
            jnp.einsum("tc,dc->td", grad_joined, qkv_full, preferred_element_type=jnp.float32)
        )
        grad_input, grad_gain_one = norm_back(
            hidden_in, inverse_one, norm_gains[layer_index, 0], grad_normed_one
        )
        grad_hidden = grad_input + grad_middle
        shards = (
            lax.psum_scatter(grad_qkv_w, "dp", scatter_dimension=0, tiled=True),
            lax.psum_scatter(grad_gu_w, "dp", scatter_dimension=0, tiled=True),
            lax.psum_scatter(grad_out_w, "dp", scatter_dimension=0, tiled=True),
            lax.psum_scatter(grad_down_w, "dp", scatter_dimension=0, tiled=True),
        )
        grad_qkv_list[layer_index] = shards[0]
        grad_gu_list[layer_index] = shards[1]
        grad_out_list[layer_index] = shards[2]
        grad_down_list[layer_index] = shards[3]
        gain_list[layer_index] = jnp.stack([grad_gain_one, grad_gain_two])
    gain_total, stat_total = lax.psum(
        (jnp.stack(gain_list), jnp.stack(stat_rows)), ("dp", "tensor")
    )
    cell_count = inputs.shape[0] * inputs.shape[1] * lax.axis_size("dp") * lax.axis_size("tensor")
    rms_values = jnp.sqrt(stat_total / cell_count)
    return (
        output,
        grad_hidden,
        jnp.stack(grad_qkv_list),
        jnp.stack(grad_gu_list),
        jnp.stack(grad_out_list),
        jnp.stack(grad_down_list),
        gain_total,
        rms_values,
    )


def solution(mesh):
    placed = (
        P(("dp", "tensor"), None),
        P(),
        P(None, "dp", "tensor"),
        P(None, "dp", None, "tensor"),
        P(None, "dp", "tensor"),
        P(None, "dp", "tensor"),
        P("dp"),
        P("dp"),
        P(("dp", "tensor"), None),
    )
    return jax.shard_map(
        per_device,
        mesh=mesh,
        in_specs=placed,
        out_specs=(
            P(("dp", "tensor"), None),
            P(("dp", "tensor"), None),
            P(None, "dp", "tensor"),
            P(None, "dp", None, "tensor"),
            P(None, "dp", "tensor"),
            P(None, "dp", "tensor"),
            P(),
            P(),
        ),
        check_vma=False,
    )
```

profile of v0, /device:TPU:0, one launch (start us, length us, event | category | flops | bytes accessed | tf_op | source)
XLA Modules:
  0.0 1162.8 jit_solution(16583962716732105338)
XLA Ops:
  11.0 2.5 multiply_convert_fusion.2
  15.8 25.8 %all-gather.21.cloned.1.call-done = bf16[1,1536,768]{2,1,0:T(8,128)(2,1)} async-done(((bf16[1,192,768]{2,1,0:T(8,128)(2,1)}), bf16[1,1536,768]{2,1,0:T(8,128)(2,1)}) %all-gather.21.cloned.1.call-update) | async-done | bytes 2359312 | tf_op jit(solution)/shard_map/all_gather | solution.py:94
  41.7 65.7 %all-gather.13.cloned.1.call-done = bf16[1024,1536]{1,0:T(8,128)(2,1)} async-done(((bf16[256,1536]{1,0:T(8,128)(2,1)}), bf16[1024,1536]{1,0:T(8,128)(2,1)}) %all-gather.13.cloned.1.call-update) | async-done | bytes 3145744 | tf_op jit(solution)/shard_map/all_gather | solution.py:53
  107.3 5.3 fusion.69
  115.7 18.8 %while.27 = (s32[]{:T(128)}, bf16[2,512,2,2,96]{1,4,3,2,0:T(8,128)(2,1)S(1)}, f32[2,2,2,512]{3,2,1,0:T(2,128)}, s32[1024]{0:T(1024)S(1)}, s32[2,512]{1,0:T(2,128...) while((s32[]{:T(128)}, ...), condition=%wide.region_4.5_spmd, body=%wide.region_1.4_spmd.sunk | while | flops 832764928 | bytes 28928132 | solution.py:130
  121.0 3.7 fusion.116
  130.1 3.7 fusion.116
  135.5 6.0 fusion.72
  142.1 108.9 %reduce-scatter.11.cloned.1.call-done = f32[256,1536]{1,0:T(8,128)} async-done(((f32[1024,1536]{1,0:T(8,128)}), f32[256,1536]{1,0:T(8,128)}) %reduce-scatter.11.cloned.1.call-update) | async-done | bytes 1572880 | tf_op jit(solution)/shard_map/reduce_scatter | solution.py:57
  251.1 2.5 multiply_reduce_fusion.9
  257.4 41.5 %all-gather.25.cloned.1.call-done = bf16[1,1536,2,1024]{3,2,0,1:T(2,128)(2,1)} async-done(((bf16[1,192,2,1024]{3,2,0,1:T(2,128)(2,1)}), bf16[1,1536,2,1024]{3,2,0,1:T(2,128)(2,1)}) %all-gather.25.cloned.1.call-update) | async-done | bytes 6291472 | tf_op jit(solution)/shard_map/all_gather | solution.py:95
  298.9 16.5 %copy.45 = bf16[1,1536,2,1024]{1,3,2,0:T(8,128)(2,1)} copy(bf16[1,1536,2,1024]{3,2,0,1:T(2,128)(2,1)} %all-gather.25.cloned.1.call-done) | data formatting | bytes 12582912 | tf_op jit(solution)/shard_map/all_gather | solution.py:95
  315.3 49.1 %all-gather.15.cloned.1.call-done = bf16[1024,1536]{1,0:T(8,128)(2,1)} async-done(((bf16[256,1536]{1,0:T(8,128)(2,1)}), bf16[1024,1536]{1,0:T(8,128)(2,1)}) %all-gather.15.cloned.1.call-update) | async-done | bytes 3145744 | tf_op jit(solution)/shard_map/all_gather | solution.py:53
  364.4 11.7 %fusion.53 = f32[1024,2,1024]{0,2,1:T(8,128)} fusion(bf16[1,1536,2,1024]{1,3,2,0:T(8,128)(2,1)} %copy.45, bf16[1024,1536]{1,0:T(8,128)(2,1)} %all-gather.15.cloned.1.call-done), kind=kOutput, calls=%fused_computation.68 | convolution fusion | flops 6442450944 | bytes 17825792 | tf_op jit(solution)/shard_map/td,dcf->tcf/dot_general | solution.py:147
  376.1 52.0 %all-gather.17.cloned.1.call-done = bf16[1024,1536]{1,0:T(8,128)(2,1)} async-done(((bf16[256,1536]{1,0:T(8,128)(2,1)}), bf16[1024,1536]{1,0:T(8,128)(2,1)}) %all-gather.17.cloned.1.call-update) | async-done | bytes 3145744 | tf_op jit(solution)/shard_map/all_gather | solution.py:61
  428.1 32.9 %all-gather.27.cloned.1.call-done = bf16[1,1536,1024]{2,1,0:T(8,128)(2,1)} async-done(((bf16[1,192,1024]{2,1,0:T(8,128)(2,1)}), bf16[1,1536,1024]{2,1,0:T(8,128)(2,1)}) %all-gather.27.cloned.1.call-update) | async-done | bytes 3145744 | tf_op jit(solution)/shard_map/all_gather | solution.py:97
  461.0 10.2 multiply_bitcast_fusion.1
  473.2 10.8 fusion.55
  484.3 5.0 multiply_convert_fusion
  490.7 5.4 fusion.63
  496.2 98.7 %reduce-scatter.15.cloned.1.call-done = f32[256,1536]{1,0:T(8,128)} async-done(((f32[1024,1536]{1,0:T(8,128)}), f32[256,1536]{1,0:T(8,128)}) %reduce-scatter.15.cloned.1.call-update) | async-done | bytes 1572880 | tf_op jit(solution)/shard_map/reduce_scatter | solution.py:65
  594.9 2.8 multiply_reduce_fusion.3
  598.4 110.0 %reduce-scatter.13.cloned.1.call-done = f32[256,1536]{1,0:T(8,128)} async-done(((f32[1024,1536]{1,0:T(8,128)}), f32[256,1536]{1,0:T(8,128)}) %reduce-scatter.13.cloned.1.call-update) | async-done | bytes 1572880 | tf_op jit(solution)/shard_map/reduce_scatter | solution.py:57
  708.4 5.4 multiply_reduce_fusion.2
  713.9 8.6 convolution_bitcast_fusion.1
  722.4 6.7 copy.69
  730.7 11.7 %fusion.58 = f32[1536,2,1024]{2,0,1:T(8,128)} fusion(bf16[1024,1536]{1,0:T(8,128)(2,1)} %all-gather.15.cloned.1.call-done, bf16[1024,1,1024]{0,2,1:T(8,128)(2,1)} %copy-done.26, bf16[1024,1,1024]{0,2,1:T(8,128)(2,1)S(1)} %copy-done.25), kind=kOutput, calls=%fused_computation.74 | convolution fusion | flops 6450839552 | bytes 19922944 | tf_op jit(solution)/shard_map/td,tc->dc/dot_general | solution.py:69
  742.5 35.5 %all-gather.19.cloned.1.call-done = bf16[1024,1536]{1,0:T(8,128)(2,1)} async-done(((bf16[256,1536]{1,0:T(8,128)(2,1)}), bf16[1024,1536]{1,0:T(8,128)(2,1)}) %all-gather.19.cloned.1.call-update) | async-done | bytes 3145744 | tf_op jit(solution)/shard_map/all_gather | solution.py:61
  778.0 4.5 convolution_convert_fusion
  782.5 4.4 reshape.429
  789.4 63.6 %while.28 = (s32[]{:T(128)}, f32[1024,2,96]{0,2,1:T(8,128)S(1)}, f32[1024,2,96]{0,2,1:T(8,128)}, f32[2,512,2,2,96]{1,0,4,3,2:T(2,128)}, bf16[2,512,2,2,96]{1,4,3...) while((s32[]{:T(128)}, f32[1024,2,96]{0,2,1:T(8,128)S(1)}, ...), condition=%wide.region_12.13_spmd.clone, body=%wide.region_10.12_spmd.clone.sunk | while | flops 2047998976 | bytes 74926256 | solution.py:291
  792.6 3.5 fusion.129
  796.1 4.2 fusion.126
  805.9 15.0 %dynamic_update_slice.20 = f32[2,512,2,2,96]{1,0,4,3,2:T(2,128)} dynamic-update-slice(f32[2,512,2,2,96]{1,0,4,3,2:T(2,128)} %get-tuple-element.557, f32[1,512,2,2,96]{1,0,4,3,2:T(1,128)S(1)} %copy.86, s32[]{:T(128)S(6)} %copy.103, s32[]{:T(128)} %constant.42.clone.1..sunk, s32[]{:T(128)} %constant.42.clone.1..sunk, s32[]{:T(128)} %constant.42.clone.1..sunk, s32[]{:T(128)} %constant.42.clone.1..sunk) | dynamic-update-slice | bytes 1572868 | tf_op jit(solution)/shard_map/while/body/jit(dynamic_update_index_in_dim)/dynamic_update_slice | solution.py:291
  823.6 4.6 fusion.129
  828.2 4.2 fusion.126
  838.0 15.0 %dynamic_update_slice.20 = f32[2,512,2,2,96]{1,0,4,3,2:T(2,128)} dynamic-update-slice(f32[2,512,2,2,96]{1,0,4,3,2:T(2,128)} %get-tuple-element.557, f32[1,512,2,2,96]{1,0,4,3,2:T(1,128)S(1)} %copy.86, s32[]{:T(128)S(6)} %copy.103, s32[]{:T(128)} %constant.42.clone.1..sunk, s32[]{:T(128)} %constant.42.clone.1..sunk, s32[]{:T(128)} %constant.42.clone.1..sunk, s32[]{:T(128)} %constant.42.clone.1..sunk) | dynamic-update-slice | bytes 1572868 | tf_op jit(solution)/shard_map/while/body/jit(dynamic_update_index_in_dim)/dynamic_update_slice | solution.py:291
  853.1 3.2 reshape.415
  860.1 4.7 fusion.67
  866.0 5.2 fusion.82
  871.3 6.8 fusion.81
  881.0 2.6 maximum_bitcast_fusion.2
  883.5 54.5 %reduce-scatter.21.cloned.1.call-done = f32[192,2,1024]{2,0,1:T(8,128)} async-done(((f32[1536,2,1024]{2,0,1:T(8,128)}), f32[192,2,1024]{2,0,1:T(8,128)}) %reduce-scatter.21.cloned.1.call-update) | async-done | bytes 1572880 | tf_op jit(solution)/shard_map/reduce_scatter | solution.py:322
  938.0 3.8 copy.53
  941.8 109.3 %reduce-scatter.17.cloned.1.call-done = f32[256,1536]{1,0:T(8,128)} async-done(((f32[1024,1536]{1,0:T(8,128)}), f32[256,1536]{1,0:T(8,128)}) %reduce-scatter.17.cloned.1.call-update) | async-done | bytes 1572880 | tf_op jit(solution)/shard_map/reduce_scatter | solution.py:65
  1052.9 41.0 %all-reduce = (f32[1,2,1536]{2,1,0:T(2,128)}, f32[1,4]{1,0:T(1,128)S(1)}) all-reduce(f32[1,2,1536]{2,1,0:T(2,128)S(1)} %maximum_bitcast_fusion.1, f32[1,4]{1,0:T(1,128)S(1)} %maximum_bitcast_fusion.2), channel_id=1, replica_groups=mesh['dp'=8,'tensor'=4] {'dp','tensor'}, use_global_device_ids=true, to_apply=%region_21.22 | all-reduce | flops 3076 | bytes 24608 | tf_op jit(solution)/shard_map/psum | solution.py:331
  1094.3 3.4 subtract_add_fusion
  1098.3 57.8 %reduce-scatter.19.cloned.1.call-done = f32[192,768]{1,0:T(8,128)} async-done(((f32[1536,768]{1,0:T(8,128)}), f32[192,768]{1,0:T(8,128)}) %reduce-scatter.19.cloned.1.call-update) | async-done | bytes 589840 | tf_op jit(solution)/shard_map/reduce_scatter | solution.py:321
  (160 shorter events, 60.7 us)
Async XLA Ops:
  7.2 7.1 copy-start.13
  7.2 7.2 copy-start.10
  7.2 34.5 %all-gather.21.cloned.1.call-start = ((), (), s32[]{:S(2)}) async-start(), calls=%async_computation.19 | async-start | bytes 2654208 | tf_op jit(solution)/shard_map/all_gather | solution.py:94
  7.9 99.4 %all-gather.13.cloned.1.call-start = ((), (), s32[]{:S(2)}) async-start(), calls=%async_computation.8 | async-start | bytes 3932160 | tf_op jit(solution)/shard_map/all_gather | solution.py:53
  8.8 5.6 copy-start.14
  8.8 245.4 %copy-start.16 = (f32[1536]{0:T(1024)}, f32[1536]{0:T(1024)S(1)}, u32[]{:S(2)}) copy-start(f32[1536]{0:T(1024)S(1)} %get-tuple-element.265) | copy-start | bytes 18436
  11.0 101.7 %copy-start.18 = (f32[256]{0:T(256)}, f32[256]{0:T(256)S(1)}, u32[]{:S(2)}) copy-start(f32[256]{0:T(256)S(1)} %get-tuple-element.347) | copy-start | bytes 3076
  13.5 122.0 %all-gather.23.cloned.1.call-start = ((), (), s32[]{:S(2)}) async-start(), calls=%async_computation.20 | async-start | bytes 1327104 | tf_op jit(solution)/shard_map/all_gather | solution.py:96
  14.2 236.8 %reduce-scatter.11.cloned.1.call-start = ((), (), s32[]{:S(2)}) async-start(), calls=%async_computation.9 | async-start | bytes 7864320 | tf_op jit(solution)/shard_map/reduce_scatter | solution.py:57
  15.8 98.0 %copy-start.4 = (f32[1024,48]{0,1:T(8,128)}, f32[1024,48]{0,1:T(8,128)S(1)}, u32[]{:S(2)}) copy-start(f32[1024,48]{0,1:T(8,128)S(1)} %get-tuple-element.345) | copy-start | bytes 589828
  135.4 6.0 copy-start.6
  141.5 109.6 %copy-start = (f32[256,1536]{1,0:T(8,128)S(1)}, f32[256,1536]{1,0:T(8,128)}, u32[]{:S(2)}) copy-start(f32[256,1536]{1,0:T(8,128)} %param.13) | copy-start | bytes 4718596
  141.5 157.4 %all-gather.25.cloned.1.call-start = ((), (), s32[]{:S(2)}) async-start(), calls=%async_computation.21 | async-start | bytes 7077888 | tf_op jit(solution)/shard_map/all_gather | solution.py:95
  142.1 222.3 %all-gather.15.cloned.1.call-start = ((), (), s32[]{:S(2)}) async-start(), calls=%async_computation.10 | async-start | bytes 3932160 | tf_op jit(solution)/shard_map/all_gather | solution.py:53
  253.6 1.1 copy-start.2
  254.2 61.1 %copy-start.20 = (f32[256]{0:T(256)}, f32[256]{0:T(256)S(1)}, u32[]{:S(2)}) copy-start(f32[256]{0:T(256)S(1)} %get-tuple-element.349) | copy-start | bytes 3076
  255.8 172.3 %all-gather.17.cloned.1.call-start = ((), (), s32[]{:S(2)}) async-start(), calls=%async_computation.12 | async-start | bytes 3932160 | tf_op jit(solution)/shard_map/all_gather | solution.py:61
  256.6 204.5 %all-gather.27.cloned.1.call-start = ((), (), s32[]{:S(2)}) async-start(), calls=%async_computation.22 | async-start | bytes 3538944 | tf_op jit(solution)/shard_map/all_gather | solution.py:97
  257.3 337.6 %reduce-scatter.15.cloned.1.call-start = ((), (), s32[]{:S(2)}) async-start(), calls=%async_computation.13 | async-start | bytes 7864320 | tf_op jit(solution)/shard_map/reduce_scatter | solution.py:65
  471.3 1.3 copy-start.24
  471.3 2.0 copy-start.26
  484.0 224.4 %reduce-scatter.13.cloned.1.call-start = ((), (), s32[]{:S(2)}) async-start(), calls=%async_computation.11 | async-start | bytes 7864320 | tf_op jit(solution)/shard_map/reduce_scatter | solution.py:57
  484.3 6.4 copy-start.22
  489.3 1.4 copy-start.9
  496.1 98.8 %copy-start.3 = (f32[256,1536]{1,0:T(8,128)S(1)}, f32[256,1536]{1,0:T(8,128)}, u32[]{:S(2)}) copy-start(f32[256,1536]{1,0:T(8,128)} %copy-done.2) | copy-start | bytes 4718596
  496.2 212.2 %copy-start.8 = (bf16[256,1536]{1,0:T(8,128)(2,1)S(1)}, bf16[256,1536]{1,0:T(8,128)(2,1)}, u32[]{:S(2)}) copy-start(bf16[256,1536]{1,0:T(8,128)(2,1)} %param.21) | copy-start | bytes 2359300
  496.2 281.8 %all-gather.19.cloned.1.call-start = ((), (), s32[]{:S(2)}) async-start(), calls=%async_computation.14 | async-start | bytes 3932160 | tf_op jit(solution)/shard_map/all_gather | solution.py:61
  713.8 164.3 %reduce-scatter.25.cloned.1.call-start = ((), (), s32[]{:S(2)}) async-start(), calls=%async_computation.23 | async-start | bytes 7077888
  729.1 1.6 copy-start.25
  729.1 208.9 %reduce-scatter.21.cloned.1.call-start = ((), (), s32[]{:S(2)}) async-start(), calls=%async_computation.17 | async-start | bytes 14155776 | tf_op jit(solution)/shard_map/reduce_scatter | solution.py:322
  742.4 35.6 %copy-start.12 = (bf16[1,1536,384]{2,1,0:T(8,128)(2,1)S(1)}, bf16[1,1536,384]{2,1,0:T(8,128)(2,1)}, u32[]{:S(2)}) copy-start(bf16[1,1536,384]{2,1,0:T(8,128)(2,1)} %all-gather.23.cloned.1.call-done) | copy-start | bytes 3538948
  742.4 308.6 %reduce-scatter.17.cloned.1.call-start = ((), (), s32[]{:S(2)}) async-start(), calls=%async_computation.15 | async-start | bytes 7864320 | tf_op jit(solution)/shard_map/reduce_scatter | solution.py:65
  853.1 3.2 copy-start.5
  853.1 3.2 copy-start.11
  857.9 2.2 copy-start.23
  864.8 1.2 copy-start.7
  864.8 233.5 %reduce-scatter.23.cloned.1.call-start = ((), (), s32[]{:S(2)}) async-start(), calls=%async_computation.18 | async-start | bytes 2654208 | tf_op jit(solution)/shard_map/reduce_scatter | solution.py:323
  871.2 284.9 %reduce-scatter.19.cloned.1.call-start = ((), (), s32[]{:S(2)}) async-start(), calls=%async_computation.16 | async-start | bytes 5308416 | tf_op jit(solution)/shard_map/reduce_scatter | solution.py:321
  878.1 2.9 copy-start.17
  878.1 172.9 %copy-start.1 = (f32[256,1536]{1,0:T(8,128)S(1)}, f32[256,1536]{1,0:T(8,128)}, u32[]{:S(2)}) copy-start(f32[256,1536]{1,0:T(8,128)} %param.13) | copy-start | bytes 4718596
  878.1 172.9 %copy-start.15 = (f32[1536]{0:T(1024)S(1)}, f32[1536]{0:T(1024)}, u32[]{:S(2)}) copy-start(f32[1536]{0:T(1024)} %copy-done.14) | copy-start | bytes 18436
  878.1 172.9 %copy-start.19 = (f32[256]{0:T(256)S(1)}, f32[256]{0:T(256)}, u32[]{:S(2)}) copy-start(f32[256]{0:T(256)} %copy-done.18) | copy-start | bytes 3076
  938.0 156.4 %copy-start.21 = (f32[256]{0:T(256)S(1)}, f32[256]{0:T(256)}, u32[]{:S(2)}) copy-start(f32[256]{0:T(256)} %get-tuple-element.346) | copy-start | bytes 3076
Sparse Core Ops, SparseCore 0:
  9.9 31.7 all-gather.20
  43.8 63.4 all-gather.12
  109.2 22.7 all-gather.22
  141.6 109.3 reduce-scatter.10
  252.8 46.0 all-gather.24
  300.9 63.4 all-gather.14
  366.0 62.1 all-gather.16
  430.0 30.9 all-gather.26
  484.2 110.7 reduce-scatter.14
  597.1 111.2 reduce-scatter.12
  713.9 64.0 all-gather.18
  781.2 60.3 reduce-scatter.24
  845.6 92.3 reduce-scatter.20
  940.2 110.7 reduce-scatter.16
  1055.2 43.1 reduce-scatter.22
  1102.2 53.8 reduce-scatter.18
where the time goes:
time: 1170 us; the launch traced here: 1160 us
  waiting for transfers between devices  846 us (72%)
  matrix products  126 us (11%)
  local copies, waits for them, and re-layouts  84.5 us (7%)
  other arithmetic  49.1 us (4%)
  blocking collectives  41 us (4%)
  between operations  14.6 us (1%)
    reduce_scatter x2, waiting for transfers between devices, collect_rows(): return lax.psum_scatter(values, 'tensor', scatter_dimension=0, tiled=True)  219 us
    reduce_scatter x2, waiting for transfers between devices, collect_grads(): return lax.psum_scatter(values, 'tensor', scatter_dimension=0, tiled=True)  208 us
    all_gather x2, waiting for transfers between devices, spread_rows(): return lax.all_gather(values, 'tensor', axis=0, tiled=True)  115 us
    all_gather x2, waiting for transfers between devices, spread_grads(): return lax.all_gather(values, 'tensor', axis=0, tiled=True)  87.5 us
    reduce_scatter x1, waiting for transfers between devices, per_device(): lax.psum_scatter(grad_qkv_w, 'dp', scatter_dimension=0, tiled=True)  57.8 us
    reduce_scatter x1, waiting for transfers between devices, per_device(): lax.psum_scatter(grad_gu_w, 'dp', scatter_dimension=0, tiled=True)  54.5 us
    all_gather x1, waiting for transfers between devices, per_device(): lax.all_gather(w_gate_up[layer_index], 'dp', axis=0, tiled=True)  41.5 us
    psum x1, blocking collectives, per_device(): lax.psum((jnp.stack(gain_list), jnp.stack(stat_rows)), ('dp', 'tensor'))  41 us
  transfers between devices with their start and end apart: 16, of which 14 were waited for; matrix products, arithmetic and copies ran while one was open for 19% of the time, Pallas kernels for 0%

commit v1 on v0

--- a/solution.py
+++ b/solution.py
@@ -1,3 +1,4 @@
+import functools
 import jax
 import jax.numpy as jnp
 from jax import lax
@@ -8,6 +9,24 @@
 HEAD_WIDTH = 96
 norm_eps = 1e-05
 rope_base = 100000.0
+
+
+def do_slot(x_part, peer_axis):
+    then = lax.axis_size(peer_axis)
+    formed = lax.axis_index(peer_axis)
+    tile_out, all_values = (then, formed)
+    newest, carry = (x_part, 1)
+    while carry < tile_out:
+        r1 = tuple(((to_i, to_i ^ carry) for to_i in range(tile_out)))
+        block_last = lax.ppermute(newest, peer_axis, r1)
+        e_now = jnp.concatenate([newest, block_last], axis=0)
+        wide_out = jnp.concatenate([block_last, newest], axis=0)
+        newest = jnp.where(all_values & carry == 0, e_now, wide_out)
+        carry = 2 * carry
+    return newest
+
+
+supply_all_lines_up = functools.partial(do_slot, peer_axis="tensor")
 
 
 def rope_tables(position, head_dim):
@@ -50,7 +69,7 @@
 
 
 def spread_rows(values):
-    return lax.all_gather(values, "tensor", axis=0, tiled=True)
+    return supply_all_lines_up(values)
 
 
 def collect_rows(values):

time: 1170 us -> 1260 us (1.077)
  waiting for transfers between devices: 846 us -> 915 us
    ppermute x0 -> x4, waiting for transfers between devices: none -> 183 us  [do_slot(): block_last = lax.ppermute(newest, peer_axis, r1)]
    all_gather x2, waiting for transfers between devices: 115 us -> 44 us  [refold(): lax.all_gather(normed_local, 'tensor', axis=0, tiled=True)]
    reduce_scatter x1, waiting for transfers between devices: 54.5 us -> 91 us  [per_device(): lax.psum_scatter(grad_gu_w, 'dp', scatter_dimension=0, tiled=True)]
    all_gather x2, waiting for transfers between devices: 87.5 us -> 51.8 us  [spread_grads(): return lax.all_gather(values, 'tensor', axis=0, tiled=True)]
    all_gather x1, waiting for transfers between devices: 25.8 us -> 0.01 us  [per_device(): lax.all_gather(w_qkv[layer_index], 'dp', axis=0, tiled=True)]
    all_gather x1, waiting for transfers between devices: 41.5 us -> 20.1 us  [per_device(): lax.all_gather(w_gate_up[layer_index], 'dp', axis=0, tiled=True)]
    unnamed x17, waiting for transfers between devices: 3.49 us -> 24.7 us
    all_gather x1, waiting for transfers between devices: 32.9 us -> 14.4 us  [per_device(): lax.all_gather(w_down[layer_index], 'dp', axis=0, tiled=True)]
  transfers between devices with their start and end apart: 16 -> 20, of which waited for: 14 -> 16; matrix products, arithmetic and copies ran while one was open for 19% -> 19% of each run, Pallas kernels for 0% -> 0%
where the time goes in v1:
time: 1260 us; the launch traced here: 1250 us
  waiting for transfers between devices  915 us (73%)
  matrix products  134 us (11%)
  local copies, waits for them, and re-layouts  85.1 us (7%)
  other arithmetic  47.4 us (4%)
  blocking collectives  41 us (3%)
  between operations  14.9 us (1%)
    reduce_scatter x2, waiting for transfers between devices, collect_rows(): return lax.psum_scatter(values, 'tensor', scatter_dimension=0, tiled=True)  220 us
    reduce_scatter x2, waiting for transfers between devices, collect_grads(): return lax.psum_scatter(values, 'tensor', scatter_dimension=0, tiled=True)  207 us
    ppermute x4, waiting for transfers between devices, do_slot(): block_last = lax.ppermute(newest, peer_axis, r1)  183 us
    reduce_scatter x1, waiting for transfers between devices, per_device(): lax.psum_scatter(grad_gu_w, 'dp', scatter_dimension=0, tiled=True)  91 us
    reduce_scatter x1, waiting for transfers between devices, per_device(): lax.psum_scatter(grad_qkv_w, 'dp', scatter_dimension=0, tiled=True)  57.8 us
    all_gather x2, waiting for transfers between devices, spread_grads(): return lax.all_gather(values, 'tensor', axis=0, tiled=True)  51.8 us
    all_gather x2, waiting for transfers between devices, refold(): lax.all_gather(normed_local, 'tensor', axis=0, tiled=True)  44 us
    psum x1, blocking collectives, per_device(): lax.psum((jnp.stack(gain_list), jnp.stack(stat_rows)), ('dp', 'tensor'))  41 us
  transfers between devices with their start and end apart: 20, of which 16 were waited for; matrix products, arithmetic and copies ran while one was open for 19% of the time, Pallas kernels for 0%

profile of v1, /device:TPU:0, one launch (start us, length us, event | category | flops | bytes accessed | tf_op | source)
XLA Modules:
  0.0 1249.9 jit_solution(9835473197070400610)
XLA Ops:
  13.1 3.1 collective-permute-start
  16.2 17.5 %collective-permute-done = bf16[256,1536]{1,0:T(8,128)(2,1)S(1)} collective-permute-done((bf16[256,1536]{1,0:T(8,128)(2,1)S(1)}, bf16[256,1536]{1,0:T(8,128)(2,1)S(1)}, u32[]{:S(2)}, u32[]{:S(2)}) %collective-permute-start) | collective-permute-done | bytes 786464 | tf_op jit(solution)/shard_map/ppermute | solution.py:21
  38.9 65.9 %collective-permute-done.1 = bf16[512,1536]{1,0:T(8,128)(2,1)} collective-permute-done((bf16[512,1536]{1,0:T(8,128)(2,1)S(1)}, bf16[512,1536]{1,0:T(8,128)(2,1)}, u32[]{:S(2)}, u32[]{:S(2)}) %collective-permute-start.1) | collective-permute-done | bytes 1572896 | tf_op jit(solution)/shard_map/ppermute | solution.py:21
  104.8 5.4 fusion.61
  112.4 17.9 %while.27 = (s32[]{:T(128)}, bf16[2,512,2,2,96]{1,4,3,2,0:T(8,128)(2,1)}, f32[2,2,2,512]{3,2,1,0:T(2,128)S(1)}, s32[1024]{0:T(1024)S(1)}, s32[2,512]{1,0:T(2,128...) while((s32[]{:T(128)}, ...), condition=%wide.region_4.5_spmd, body=%wide.region_1.4_spmd.sunk | while | flops 832764928 | bytes 35219636 | solution.py:149
  117.5 3.1 fusion.130
  126.3 3.1 fusion.130
  132.6 6.0 fusion.85
  140.4 110.1 %reduce-scatter.11.cloned.1.call-done = f32[256,1536]{1,0:T(8,128)} async-done(((f32[1024,1536]{1,0:T(8,128)}), f32[256,1536]{1,0:T(8,128)}) %reduce-scatter.11.cloned.1.call-update) | async-done | bytes 1572880 | tf_op jit(solution)/shard_map/reduce_scatter | solution.py:76
  256.7 17.8 %collective-permute-done.2 = bf16[256,1536]{1,0:T(8,128)(2,1)S(1)} collective-permute-done((bf16[256,1536]{1,0:T(8,128)(2,1)S(1)}, bf16[256,1536]{1,0:T(8,128)(2,1)S(1)}, u32[]{:S(2)}, u32[]{:S(2)}) %collective-permute-start.2) | collective-permute-done | bytes 786464 | tf_op jit(solution)/shard_map/ppermute | solution.py:21
  278.2 20.1 %all-gather.25.cloned.1.call-done = bf16[1,1536,2,1024]{3,2,0,1:T(2,128)(2,1)} async-done(((bf16[1,192,2,1024]{3,2,0,1:T(2,128)(2,1)}), bf16[1,1536,2,1024]{3,2,0,1:T(2,128)(2,1)}) %all-gather.25.cloned.1.call-update) | async-done | bytes 6291472 | tf_op jit(solution)/shard_map/all_gather | solution.py:114
  298.3 16.6 %copy.45 = bf16[1,1536,2,1024]{1,3,2,0:T(8,128)(2,1)} copy(bf16[1,1536,2,1024]{3,2,0,1:T(2,128)(2,1)} %all-gather.25.cloned.1.call-done) | data formatting | bytes 12582912 | tf_op jit(solution)/shard_map/all_gather | solution.py:114
  314.9 81.7 %collective-permute-done.3 = bf16[512,1536]{1,0:T(8,128)(2,1)} collective-permute-done((bf16[512,1536]{1,0:T(8,128)(2,1)S(1)}, bf16[512,1536]{1,0:T(8,128)(2,1)}, u32[]{:S(2)}, u32[]{:S(2)}) %collective-permute-start.3) | collective-permute-done | bytes 1572896 | tf_op jit(solution)/shard_map/ppermute | solution.py:21
  396.6 12.7 %fusion.53 = f32[1024,2,1024]{0,2,1:T(8,128)} fusion(bf16[1,1536,2,1024]{1,3,2,0:T(8,128)(2,1)} %copy.45, bf16[512,1536]{1,0:T(8,128)(2,1)} %collective-permute-done.3, bf16[512,1536]{1,0:T(8,128)(2,1)S(1)} %maximum_select_fusion.4, pred[]{:T(512)S(6)} %eq.62), kind=kOutput, calls=%fused_computation.68 | convolution fusion | flops 6456606720 | bytes 17825792 | tf_op jit(solution)/shard_map/td,dcf->tcf/dot_general | solution.py:166
  409.3 14.4 %all-gather.27.cloned.1.call-done = bf16[1,1536,1024]{2,1,0:T(8,128)(2,1)} async-done(((bf16[1,192,1024]{2,1,0:T(8,128)(2,1)}), bf16[1,1536,1024]{2,1,0:T(8,128)(2,1)}) %all-gather.27.cloned.1.call-update) | async-done | bytes 3145744 | tf_op jit(solution)/shard_map/all_gather | solution.py:116
  423.7 10.3 multiply_bitcast_fusion.1
  436.0 10.7 fusion.55
  447.0 5.0 multiply_convert_fusion
  453.4 5.5 fusion.77
  459.7 98.0 %reduce-scatter.15.cloned.1.call-done = f32[256,1536]{1,0:T(8,128)} async-done(((f32[1024,1536]{1,0:T(8,128)}), f32[256,1536]{1,0:T(8,128)}) %reduce-scatter.15.cloned.1.call-update) | async-done | bytes 1572880 | tf_op jit(solution)/shard_map/reduce_scatter | solution.py:84
  561.0 110.2 %reduce-scatter.13.cloned.1.call-done = f32[256,1536]{1,0:T(8,128)} async-done(((f32[1024,1536]{1,0:T(8,128)}), f32[256,1536]{1,0:T(8,128)}) %reduce-scatter.13.cloned.1.call-update) | async-done | bytes 1572880 | tf_op jit(solution)/shard_map/reduce_scatter | solution.py:76
  671.3 5.5 multiply_reduce_fusion.2
  677.5 8.7 convolution_bitcast_fusion.1
  686.2 6.7 copy.69
  692.9 44.0 %all-gather.19.cloned.1.call-done = bf16[1024,1536]{1,0:T(8,128)(2,1)} async-done(((bf16[256,1536]{1,0:T(8,128)(2,1)}), bf16[1024,1536]{1,0:T(8,128)(2,1)}) %all-gather.19.cloned.1.call-update) | async-done | bytes 3145744 | tf_op jit(solution)/shard_map/all_gather | solution.py:90
  736.9 12.2 fusion.58
  749.3 51.8 %all-gather.15.cloned.1.call-done = bf16[1024,1536]{1,0:T(8,128)(2,1)} async-done(((bf16[256,1536]{1,0:T(8,128)(2,1)}), bf16[1024,1536]{1,0:T(8,128)(2,1)}) %all-gather.15.cloned.1.call-update) | async-done | bytes 3145744 | tf_op jit(solution)/shard_map/all_gather | solution.py:80
  801.1 4.6 convolution_convert_fusion
  805.6 4.5 reshape.429
  810.1 3.6 copy.50
  813.7 70.1 %while.28 = (s32[]{:T(128)}, f32[1024,2,96]{0,2,1:T(8,128)S(1)}, f32[1024,2,96]{0,2,1:T(8,128)}, f32[2,512,2,2,96]{1,0,4,3,2:T(2,128)}, bf16[2,512,2,2,96]{1,4,3...) while((s32[]{:T(128)}, f32[1024,2,96]{0,2,1:T(8,128)S(1)}, ...), condition=%wide.region_12.13_spmd.clone, body=%wide.region_10.12_spmd.clone.sunk | while | flops 2047998976 | bytes 133122368 | solution.py:310
  815.9 3.2 fusion.140
  823.9 15.0 %dynamic_update_slice.20 = f32[2,512,2,2,96]{1,0,4,3,2:T(2,128)} dynamic-update-slice(f32[2,512,2,2,96]{1,0,4,3,2:T(2,128)} %get-tuple-element.557, f32[1,512,2,2,96]{1,0,4,3,2:T(1,128)S(1)} %copy.86, s32[]{:T(128)} %get-tuple-element.554, s32[]{:T(128)} %constant.43.clone.1..sunk, s32[]{:T(128)} %constant.43.clone.1..sunk, s32[]{:T(128)} %constant.43.clone.1..sunk, s32[]{:T(128)} %constant.43.clone.1..sunk) | dynamic-update-slice | bytes 1572868 | tf_op jit(solution)/shard_map/while/body/jit(dynamic_update_index_in_dim)/dynamic_update_slice | solution.py:310
  838.9 3.2 fusion.142
  842.1 5.8 fusion.143
  849.9 3.2 fusion.140
  857.8 15.0 %dynamic_update_slice.20 = f32[2,512,2,2,96]{1,0,4,3,2:T(2,128)} dynamic-update-slice(f32[2,512,2,2,96]{1,0,4,3,2:T(2,128)} %get-tuple-element.557, f32[1,512,2,2,96]{1,0,4,3,2:T(1,128)S(1)} %copy.86, s32[]{:T(128)} %get-tuple-element.554, s32[]{:T(128)} %constant.43.clone.1..sunk, s32[]{:T(128)} %constant.43.clone.1..sunk, s32[]{:T(128)} %constant.43.clone.1..sunk, s32[]{:T(128)} %constant.43.clone.1..sunk) | dynamic-update-slice | bytes 1572868 | tf_op jit(solution)/shard_map/while/body/jit(dynamic_update_index_in_dim)/dynamic_update_slice | solution.py:310
  872.8 3.6 fusion.142
  876.5 7.3 fusion.143
  889.8 4.6 fusion.81
  895.5 5.2 fusion.97
  900.8 6.7 fusion.96
  907.6 21.0 %reduce-scatter.25.cloned.1.call-done = f32[192,1024]{1,0:T(8,128)} async-done(((f32[1536,1024]{1,0:T(8,128)}), f32[192,1024]{1,0:T(8,128)}) %reduce-scatter.25.cloned.1.call-update) | async-done | bytes 786448
  933.8 91.0 %reduce-scatter.21.cloned.1.call-done = f32[192,2,1024]{2,0,1:T(8,128)} async-done(((f32[1536,2,1024]{2,0,1:T(8,128)}), f32[192,2,1024]{2,0,1:T(8,128)}) %reduce-scatter.21.cloned.1.call-update) | async-done | bytes 1572880 | tf_op jit(solution)/shard_map/reduce_scatter | solution.py:341
  1024.8 3.9 copy.53
  1028.7 109.1 %reduce-scatter.17.cloned.1.call-done = f32[256,1536]{1,0:T(8,128)} async-done(((f32[1024,1536]{1,0:T(8,128)}), f32[256,1536]{1,0:T(8,128)}) %reduce-scatter.17.cloned.1.call-update) | async-done | bytes 1572880 | tf_op jit(solution)/shard_map/reduce_scatter | solution.py:84
  1139.7 41.0 %all-reduce = (f32[1,2,1536]{2,1,0:T(2,128)}, f32[1,4]{1,0:T(1,128)S(1)}) all-reduce(f32[1,2,1536]{2,1,0:T(2,128)S(1)} %maximum_bitcast_fusion.1, f32[1,4]{1,0:T(1,128)S(1)} %maximum_bitcast_fusion.2), channel_id=1, replica_groups=mesh['dp'=8,'tensor'=4] {'dp','tensor'}, use_global_device_ids=true, to_apply=%region_21.22 | all-reduce | flops 3076 | bytes 24608 | tf_op jit(solution)/shard_map/psum | solution.py:350
  1185.2 57.8 %reduce-scatter.19.cloned.1.call-done = f32[192,768]{1,0:T(8,128)} async-done(((f32[1536,768]{1,0:T(8,128)}), f32[192,768]{1,0:T(8,128)}) %reduce-scatter.19.cloned.1.call-update) | async-done | bytes 589840 | tf_op jit(solution)/shard_map/reduce_scatter | solution.py:340
  (208 shorter events, 79.0 us)
Async XLA Ops:
  7.2 97.6 %all-gather.21.cloned.1.call-start = ((), (), s32[]{:S(2)}) async-start(), calls=%async_computation.19 | async-start | bytes 2654208 | tf_op jit(solution)/shard_map/all_gather | solution.py:113
  7.9 124.7 %all-gather.23.cloned.1.call-start = ((), (), s32[]{:S(2)}) async-start(), calls=%async_computation.20 | async-start | bytes 1327104 | tf_op jit(solution)/shard_map/all_gather | solution.py:115
  9.4 25.0 %copy-start.26 = (f32[1536]{0:T(1024)}, f32[1536]{0:T(1024)S(1)}, u32[]{:S(2)}) copy-start(f32[1536]{0:T(1024)S(1)} %get-tuple-element.266) | copy-start | bytes 18436
  11.0 26.3 %copy-start.25 = (s32[1024]{0:T(1024)S(1)}, s32[1024]{0:T(1024)}, u32[]{:S(2)}) copy-start(s32[1024]{0:T(1024)} %param.20) | copy-start | bytes 12292
  11.0 26.4 %copy-start.20 = (s32[1024]{0:T(1024)S(1)}, s32[1024]{0:T(1024)}, u32[]{:S(2)}) copy-start(s32[1024]{0:T(1024)} %param.19) | copy-start | bytes 12292
  11.5 25.9 %copy-start.31 = (f32[256]{0:T(256)}, f32[256]{0:T(256)S(1)}, u32[]{:S(2)}) copy-start(f32[256]{0:T(256)S(1)} %get-tuple-element.347) | copy-start | bytes 3076
  13.1 97.0 %copy-start.11 = (bf16[256,1536]{1,0:T(8,128)(2,1)}, bf16[256,1536]{1,0:T(8,128)(2,1)S(1)}, u32[]{:S(2)}) copy-start(bf16[256,1536]{1,0:T(8,128)(2,1)S(1)} %multiply_convert_fusion.2) | copy-start | bytes 2359300
  13.1 20.6 %collective-permute-start = (bf16[256,1536]{1,0:T(8,128)(2,1)S(1)}, bf16[256,1536]{1,0:T(8,128)(2,1)S(1)}, u32[]{:S(2)}, u32[]{:S(2)}) collective-permute-start(bf16[256,1536]{1,0:T(8,128)(2,1)S(1)} %multiply_convert_fusion.2), channel_id=1, source_target_pairs={{0,1},{1,0},{2,3},{3,2},{4,5},{5,4},{6,7},{7,6},{8,9},{9,8},{10,11... | collective-permute-start | bytes 2359304 | tf_op jit(solution)/shard_map/ppermute | solution.py:21
  34.4 70.4 %collective-permute-start.1 = (bf16[512,1536]{1,0:T(8,128)(2,1)S(1)}, bf16[512,1536]{1,0:T(8,128)(2,1)}, u32[]{:S(2)}, u32[]{:S(2)}) collective-permute-start(bf16[512,1536]{1,0:T(8,128)(2,1)S(1)} %maximum_select_fusion.3), channel_id=1, source_target_pairs={{0,2},{1,3},{2,0},{3,1},{4,6},{5,7},{6,4},{7,5},{8,10},{9,11},{10,... | collective-permute-start | bytes 4718600 | tf_op jit(solution)/shard_map/ppermute | solution.py:21
  37.3 213.2 %reduce-scatter.11.cloned.1.call-start = ((), (), s32[]{:S(2)}) async-start(), calls=%async_computation.8 | async-start | bytes 7864320 | tf_op jit(solution)/shard_map/reduce_scatter | solution.py:76
  38.9 71.7 %copy-start.14 = (f32[1024,48]{0,1:T(8,128)}, f32[1024,48]{0,1:T(8,128)S(1)}, u32[]{:S(2)}) copy-start(f32[1024,48]{0,1:T(8,128)S(1)} %get-tuple-element.345) | copy-start | bytes 589828
  130.3 8.2 copy-start.6
  130.3 8.2 copy-start.28
  132.5 6.0 copy-start.16
  138.6 111.9 %copy-start.2 = (f32[256,1536]{1,0:T(8,128)S(1)}, f32[256,1536]{1,0:T(8,128)}, u32[]{:S(2)}) copy-start(f32[256,1536]{1,0:T(8,128)} %param.13) | copy-start | bytes 4718596
  138.6 159.7 %all-gather.25.cloned.1.call-start = ((), (), s32[]{:S(2)}) async-start(), calls=%async_computation.21 | async-start | bytes 7077888 | tf_op jit(solution)/shard_map/all_gather | solution.py:114
  139.2 270.1 %all-gather.13.cloned.1.call-start = ((), (), s32[]{:S(2)}) async-start(), calls=%async_computation.10 | async-start | bytes 3932160 | tf_op jit(solution)/shard_map/all_gather | solution.py:80
  139.8 284.0 %all-gather.27.cloned.1.call-start = ((), (), s32[]{:S(2)}) async-start(), calls=%async_computation.22 | async-start | bytes 3538944 | tf_op jit(solution)/shard_map/all_gather | solution.py:116
  140.3 417.3 %reduce-scatter.15.cloned.1.call-start = ((), (), s32[]{:S(2)}) async-start(), calls=%async_computation.11 | async-start | bytes 7864320 | tf_op jit(solution)/shard_map/reduce_scatter | solution.py:84
  255.1 59.8 %copy-start.12 = (bf16[256,1536]{1,0:T(8,128)(2,1)}, bf16[256,1536]{1,0:T(8,128)(2,1)S(1)}, u32[]{:S(2)}) copy-start(bf16[256,1536]{1,0:T(8,128)(2,1)S(1)} %multiply_convert_fusion.1) | copy-start | bytes 2359300
  255.1 19.4 %collective-permute-start.2 = (bf16[256,1536]{1,0:T(8,128)(2,1)S(1)}, bf16[256,1536]{1,0:T(8,128)(2,1)S(1)}, u32[]{:S(2)}, u32[]{:S(2)}) collective-permute-start(bf16[256,1536]{1,0:T(8,128)(2,1)S(1)} %multiply_convert_fusion.1), channel_id=1, source_target_pairs={{0,1},{1,0},{2,3},{3,2},{4,5},{5,4},{6,7},{7,6},{8,9},{9,8},{10,11... | collective-permute-start | bytes 2359304 | tf_op jit(solution)/shard_map/ppermute | solution.py:21
  275.2 121.4 %collective-permute-start.3 = (bf16[512,1536]{1,0:T(8,128)(2,1)S(1)}, bf16[512,1536]{1,0:T(8,128)(2,1)}, u32[]{:S(2)}, u32[]{:S(2)}) collective-permute-start(bf16[512,1536]{1,0:T(8,128)(2,1)S(1)} %maximum_select_fusion.4), channel_id=1, source_target_pairs={{0,2},{1,3},{2,0},{3,1},{4,6},{5,7},{6,4},{7,5},{8,10},{9,11},{10,... | collective-permute-start | bytes 4718600 | tf_op jit(solution)/shard_map/ppermute | solution.py:21
  446.8 224.5 %reduce-scatter.13.cloned.1.call-start = ((), (), s32[]{:S(2)}) async-start(), calls=%async_computation.9 | async-start | bytes 7864320 | tf_op jit(solution)/shard_map/reduce_scatter | solution.py:76
  447.0 6.4 copy-start.35
  458.9 98.8 %copy-start.5 = (f32[256,1536]{1,0:T(8,128)S(1)}, f32[256,1536]{1,0:T(8,128)}, u32[]{:S(2)}) copy-start(f32[256,1536]{1,0:T(8,128)} %copy-done.4) | copy-start | bytes 4718596
  458.9 212.4 %copy-start.18 = (bf16[256,1536]{1,0:T(8,128)(2,1)S(1)}, bf16[256,1536]{1,0:T(8,128)(2,1)}, u32[]{:S(2)}) copy-start(bf16[256,1536]{1,0:T(8,128)(2,1)} %param.21) | copy-start | bytes 2359300
  458.9 278.0 %all-gather.19.cloned.1.call-start = ((), (), s32[]{:S(2)}) async-start(), calls=%async_computation.16 | async-start | bytes 3932160 | tf_op jit(solution)/shard_map/all_gather | solution.py:90
  459.6 341.5 %all-gather.15.cloned.1.call-start = ((), (), s32[]{:S(2)}) async-start(), calls=%async_computation.12 | async-start | bytes 3932160 | tf_op jit(solution)/shard_map/all_gather | solution.py:80
  676.8 224.0 %all-gather.17.cloned.1.call-start = ((), (), s32[]{:S(2)}) async-start(), calls=%async_computation.14 | async-start | bytes 3932160 | tf_op jit(solution)/shard_map/all_gather | solution.py:90
  677.5 251.0 %reduce-scatter.25.cloned.1.call-start = ((), (), s32[]{:S(2)}) async-start(), calls=%async_computation.23 | async-start | bytes 7077888
  692.9 332.0 %reduce-scatter.21.cloned.1.call-start = ((), (), s32[]{:S(2)}) async-start(), calls=%async_computation.17 | async-start | bytes 14155776 | tf_op jit(solution)/shard_map/reduce_scatter | solution.py:341
  749.2 51.9 %copy-start.22 = (bf16[1,1536,384]{2,1,0:T(8,128)(2,1)S(1)}, bf16[1,1536,384]{2,1,0:T(8,128)(2,1)}, u32[]{:S(2)}) copy-start(bf16[1,1536,384]{2,1,0:T(8,128)(2,1)} %all-gather.23.cloned.1.call-done) | copy-start | bytes 3538948
  749.2 388.7 %reduce-scatter.17.cloned.1.call-start = ((), (), s32[]{:S(2)}) async-start(), calls=%async_computation.13 | async-start | bytes 7864320 | tf_op jit(solution)/shard_map/reduce_scatter | solution.py:84
  805.6 8.1 copy-start.7
  805.6 8.1 copy-start.29
  815.9 3.3 copy-start
  842.1 5.8 copy-start.8
  849.8 3.3 copy-start
  872.8 3.6 copy-start.10
  876.5 7.3 copy-start.8
  894.4 290.7 %reduce-scatter.23.cloned.1.call-start = ((), (), s32[]{:S(2)}) async-start(), calls=%async_computation.18 | async-start | bytes 2654208 | tf_op jit(solution)/shard_map/reduce_scatter | solution.py:342
  900.7 342.2 %reduce-scatter.19.cloned.1.call-start = ((), (), s32[]{:S(2)}) async-start(), calls=%async_computation.15 | async-start | bytes 5308416 | tf_op jit(solution)/shard_map/reduce_scatter | solution.py:340
  907.5 23.7 %copy-start.30 = (f32[1536]{0:T(1024)S(1)}, f32[1536]{0:T(1024)}, u32[]{:S(2)}) copy-start(f32[1536]{0:T(1024)} %get-tuple-element.262) | copy-start | bytes 18436
  907.5 230.4 %copy-start.3 = (f32[256,1536]{1,0:T(8,128)S(1)}, f32[256,1536]{1,0:T(8,128)}, u32[]{:S(2)}) copy-start(f32[256,1536]{1,0:T(8,128)} %param.13) | copy-start | bytes 4718596
  907.5 230.3 %copy-start.27 = (f32[1536]{0:T(1024)S(1)}, f32[1536]{0:T(1024)}, u32[]{:S(2)}) copy-start(f32[1536]{0:T(1024)} %copy-done.26) | copy-start | bytes 18436
  907.5 230.3 %copy-start.32 = (f32[256]{0:T(256)S(1)}, f32[256]{0:T(256)}, u32[]{:S(2)}) copy-start(f32[256]{0:T(256)} %copy-done.31) | copy-start | bytes 3076
  1024.8 156.4 %copy-start.13 = (f32[256,1536]{1,0:T(8,128)S(1)}, f32[256,1536]{1,0:T(8,128)}, u32[]{:S(2)}) copy-start(f32[256,1536]{1,0:T(8,128)} %get-tuple-element.338) | copy-start | bytes 4718596
  1024.8 156.4 %copy-start.34 = (f32[256]{0:T(256)S(1)}, f32[256]{0:T(256)}, u32[]{:S(2)}) copy-start(f32[256]{0:T(256)} %get-tuple-element.346) | copy-start | bytes 3076
  (18 other events, 32.3 us)
Sparse Core Ops, SparseCore 0:
  9.9 31.7 all-gather.20
  43.5 24.0 all-gather.22
  138.7 111.7 reduce-scatter.10
  252.2 46.0 all-gather.24
  299.7 89.3 all-gather.12
  390.9 32.8 all-gather.26
  446.9 110.7 reduce-scatter.14
  560.0 111.2 reduce-scatter.12
  672.8 64.0 all-gather.18
  738.9 62.1 all-gather.14
  802.7 62.1 all-gather.16
  868.1 60.3 reduce-scatter.24
  932.4 92.3 reduce-scatter.20
  1027.1 110.7 reduce-scatter.16
  1142.0 43.1 reduce-scatter.22
  1189.0 53.8 reduce-scatter.18
